TPU v7x, 256 devices: a whole 4x4x8 slice. The times are simulated.
256 devices in a mesh: section: 8 (over y, x_lo), dp: 32 (over x_hi, z, core).
Axes of the slice: x: 4 (x_hi: 2, x_lo: 2; x = x_hi * 2 + x_lo), y: 4, z: 8, core: 2. Of those that a mesh axis runs over, the one named last changes fastest.
Arguments:
- images: bfloat16 [4, 6144, 512], P(None, 'dp'), may hold values from -6 to 6
- out_grad: bfloat16 [4, 6144, 512], P(None, 'dp'), may hold values from -0.0390625 to 0.0390625
- w_in: bfloat16 [8, 2, 512, 512], P('section'), may hold values from -0.25 to 0.25
- w_out: bfloat16 [8, 2, 512, 512], P('section'), may hold values from -0.25 to 0.25
Outputs:
- grad_in: float32 [8, 2, 512, 512], P('section', None, 'dp')
- grad_out: float32 [8, 2, 512, 512], P('section', None, 'dp')
All inputs are finite; a program needn't handle non-finite values.
Results may differ from a plain program's by a relative error of at most 0.04.
Values may be sent and summed in bfloat16 or wider, within the bound.
A program may use at most 64 MiB of HBM per device.

v0:
```python
import jax
import jax.numpy as jnp
from jax import lax
from jax.sharding import PartitionSpec as P

norm_epsilon = 1e-06


def passed_along(value, axis, steps):
    count = lax.axis_size(axis)
    first, last = (max(0, -steps), min(count, count - steps))
    return lax.ppermute(value, axis, [(source, source + steps) for source in range(first, last)])


def norm_scale(values):
    return lax.rsqrt(jnp.mean(values * values, axis=-1, keepdims=True) + norm_epsilon)


def cell_forward(current, weight_in, weight_out):
    wide = current.astype(jnp.float32)
    scale = norm_scale(wide)
    normed = (wide * scale).astype(jnp.bfloat16)
    pre_act = jnp.dot(normed, weight_in, preferred_element_type=jnp.float32)
    hidden = jax.nn.silu(pre_act).astype(jnp.bfloat16)
    result = (wide + jnp.dot(hidden, weight_out, preferred_element_type=jnp.float32)).astype(
        jnp.bfloat16
    )
    return (result, (normed, pre_act, hidden))


def cell_backward(grad_y, current, retained, weight_in, weight_out):
    normed, pre_act, hidden = retained
    grad_wout = jnp.dot(hidden.T, grad_y, preferred_element_type=jnp.float32)
    grad_hidden = jnp.dot(grad_y, weight_out.T, preferred_element_type=jnp.float32)
    sigmoid_act = jax.nn.sigmoid(pre_act)
    grad_pre = (grad_hidden * sigmoid_act * (1.0 + pre_act * (1.0 - sigmoid_act))).astype(
        jnp.bfloat16
    )
    grad_win = jnp.dot(normed.T, grad_pre, preferred_element_type=jnp.float32)
    grad_normed = jnp.dot(grad_pre, weight_in.T, preferred_element_type=jnp.float32)
    wide = current.astype(jnp.float32)
    scale = norm_scale(wide)
    grad_wide = scale * (
        grad_normed - wide * scale * scale * jnp.mean(grad_normed * wide, axis=-1, keepdims=True)
    )
    return ((grad_y.astype(jnp.float32) + grad_wide).astype(jnp.bfloat16), grad_win, grad_wout)


def section_forward(current, weight_in, weight_out):
    inputs, normeds, pre_acts, hiddens = ([], [], [], [])
    for cell_index in range(weight_in.shape[0]):
        inputs.append(current)
        current, retained = cell_forward(current, weight_in[cell_index], weight_out[cell_index])
        normeds.append(retained[0])
        pre_acts.append(retained[1])
        hiddens.append(retained[2])
    return (
        current,
        (jnp.stack(inputs), jnp.stack(normeds), jnp.stack(pre_acts), jnp.stack(hiddens)),
    )


def cell_grads(grad_y, saved, cell_index, weight_in, weight_out):
    retained = (saved[1][cell_index], saved[2][cell_index], saved[3][cell_index])
    return cell_backward(
        grad_y, saved[0][cell_index], retained, weight_in[cell_index], weight_out[cell_index]
    )


def read_slot(whole, slot_index):
    return lax.dynamic_index_in_dim(whole, slot_index, 0, keepdims=False)


def own_rows(summed):
    share = summed.shape[1] // lax.axis_size("dp")
    return lax.dynamic_slice_in_dim(summed, lax.axis_index("dp") * share, share, 1)


def section_reduce(total_in, total_out):
    summed_in, summed_out = (
        lax.psum(total_in.astype(jnp.bfloat16), "dp").astype(jnp.float32),
        lax.psum(total_out.astype(jnp.bfloat16), "dp").astype(jnp.float32),
    )
    return (own_rows(summed_in), own_rows(summed_out))


def local(images, out_grad, w_in, w_out):
    weight_in = w_in[0]
    weight_out = w_out[0]
    cell_count = weight_in.shape[0]
    micro_count, row_count, channels = images.shape
    section_count = lax.axis_size("section")
    position = lax.axis_index("section")
    step_count = micro_count + section_count - 1
    zero_act = jnp.zeros((row_count, channels), jnp.bfloat16)
    stored = (
        jnp.zeros((micro_count, cell_count, row_count, channels), jnp.bfloat16),
        jnp.zeros((micro_count, cell_count, row_count, channels), jnp.bfloat16),
        jnp.zeros((micro_count, cell_count, row_count, channels), jnp.float32),
        jnp.zeros((micro_count, cell_count, row_count, channels), jnp.bfloat16),
    )

    def forward_step(tick_index, carry):
        incoming, stored = carry
        micro_index = tick_index - position
        active = (micro_index >= 0) & (micro_index < micro_count)
        slot_index = jnp.clip(micro_index, 0, micro_count - 1)
        current = jnp.where(position == 0, read_slot(images, slot_index), incoming)
        result, saved = section_forward(current, weight_in, weight_out)

        def put_slot(whole, fresh):
            chosen = jnp.where(active, fresh, read_slot(whole, slot_index))
            return lax.dynamic_update_index_in_dim(whole, chosen, slot_index, 0)

        stored = jax.tree.map(put_slot, stored, saved)
        outgoing = passed_along(result, "section", 1)
        return (outgoing, stored)

    unused_act, stored = lax.fori_loop(0, step_count, forward_step, (zero_act, stored))

    def saved_for(slot_index):
        return tuple((read_slot(whole, slot_index) for whole in stored))

    def backward_input(tick_index, incoming):
        micro_index = tick_index - (section_count - 1 - position)
        active = (micro_index >= 0) & (micro_index < micro_count)
        slot_index = jnp.clip(micro_index, 0, micro_count - 1)
        grad_y = jnp.where(position == section_count - 1, read_slot(out_grad, slot_index), incoming)
        return (grad_y, slot_index, active)

    def backward_step(tick_index, carry):
        incoming, total_in, total_out = carry
        grad_y, slot_index, active = backward_input(tick_index, incoming)
        saved = saved_for(slot_index)
        grads_in = [None] * cell_count
        grads_out = [None] * cell_count
        for cell_index in reversed(range(cell_count)):
            grad_y, grads_in[cell_index], grads_out[cell_index] = cell_grads(
                grad_y, saved, cell_index, weight_in, weight_out
            )
        total_in = total_in + jnp.where(active, jnp.stack(grads_in), 0.0)
        total_out = total_out + jnp.where(active, jnp.stack(grads_out), 0.0)
        outgoing = passed_along(grad_y, "section", -1)
        return (outgoing, total_in, total_out)

    zero_grads = jnp.zeros((cell_count, channels, channels), jnp.float32)
    unused_grad, total_in, total_out = lax.fori_loop(
        0, step_count, backward_step, (zero_act, zero_grads, zero_grads)
    )
    summed_in, summed_out = section_reduce(total_in, total_out)
    return (summed_in[None], summed_out[None])


def solution(mesh):
    return jax.shard_map(
        local,
        mesh=mesh,
        in_specs=(
            P(None, "dp", None),
            P(None, "dp", None),
            P("section", None, None, None),
            P("section", None, None, None),
        ),
        out_specs=(P("section", None, "dp", None), P("section", None, "dp", None)),
        check_vma=False,
    )
```

profile of v0, /device:TPU:1, one launch (start us, length us, event | category | flops | bytes accessed | tf_op | source)
XLA Modules:
  0.0 748.4 jit_solution(3749055273018448880)
XLA Ops:
  13.3 176.5 %while.42 = (s32[]{:T(128)}, bf16[192,512]{1,0:T(8,128)(2,1)S(1)}, bf16[4,2,192,512]{3,2,1,0:T(8,128)(2,1)}, bf16[4,2,192,512]{3,2,1,0:T(8,128)(2,1)}, f32[4,2,1...) while((s32[]{:T(128)}, bf16[192,512]{1,0:T(8,128)(2,1)S(1)}, ...), condition=%wide.region_3.4_spmd, body=%wide.region_0.3_spmd.sunk | while | flops 410419584 | bytes 14098178 | solution.py:119
  19.9 4.0 collective-permute-start
  37.1 3.2 collective-permute-start
  53.6 3.2 collective-permute-start
  70.1 3.1 collective-permute-start
  86.5 3.2 collective-permute-start
  103.0 2.8 collective-permute-start
  119.0 3.2 collective-permute-start
  189.8 254.2 %while.43 = (s32[]{:T(128)}, bf16[192,512]{1,0:T(8,128)(2,1)S(1)}, f32[2,512,512]{2,1,0:T(8,128)}, f32[2,512,512]{2,1,0:T(8,128)}, pred[]{:T(512)}, /*index=5*/s...) while((s32[]{:T(128)}, bf16[192,512]{1,0:T(8,128)(2,1)S(1)}, ...), condition=%wide.region_9.10_spmd.clone, body=%wide.region_4.9_spmd.clone.sunk | while | flops 814219648 | bytes 28717460 | solution.py:147
  205.2 2.3 convolution_bitcast_fusion.8
  207.5 4.3 fusion.135
  227.1 2.3 convolution_bitcast_fusion.8
  229.4 5.6 fusion.135
  250.3 2.3 convolution_bitcast_fusion.8
  252.6 5.6 fusion.135
  273.5 2.3 convolution_bitcast_fusion.8
  275.8 5.6 fusion.135
  296.8 2.3 convolution_bitcast_fusion.8
  299.1 5.6 fusion.135
  320.0 2.3 convolution_bitcast_fusion.8
  322.3 5.6 fusion.135
  343.2 2.3 convolution_bitcast_fusion.8
  345.5 5.6 fusion.135
  366.4 2.3 convolution_bitcast_fusion.8
  368.7 5.6 fusion.135
  392.0 5.6 fusion.135
  412.9 2.3 convolution_bitcast_fusion.8
  415.2 5.6 fusion.135
  436.1 2.3 convolution_bitcast_fusion.8
  438.4 5.6 fusion.135
  444.0 2.9 convert_element_type.154
  448.0 292.1 %all-reduce.3.cloned.1.call-done = (bf16[2,512,512]{2,1,0:T(8,128)(2,1)}, bf16[2,512,512]{2,1,0:T(8,128)(2,1)}) async-done(((bf16[2,512,512]{2,1,0:T(8,128)(2,1)}, bf16[2,512,512]{2,1,0:T(8,128)(2,1)}), (bf16[2,512,512]{2,1,0:T(8,128)(2,1)}, bf16[2,512,512]{2,1,0:T(8,128)(2,1)})) %all-reduce.3.cloned.1.call-update) | async-done | bytes 2097168 | tf_op jit(solution)/shard_map/psum | solution.py:81
  (382 shorter events, 331.4 us)
Async XLA Ops:
  7.2 733.0 %all-reduce.3.cloned.1.call-start = ((), (), s32[]{:S(2)}) async-start(), calls=%async_computation | async-start | bytes 4194304 | tf_op jit(solution)/shard_map/psum | solution.py:81
  19.9 10.7 %collective-permute-start = (bf16[192,512]{1,0:T(8,128)(2,1)S(1)}, bf16[192,512]{1,0:T(8,128)(2,1)S(1)}, u32[]{:S(2)}, u32[]{:S(2)}) collective-permute-start(bf16[192,512]{1,0:T(8,128)(2,1)S(1)} %fusion.112), channel_id=1, source_target_pairs={{0,32},{32,64},{64,96},{96,128},{128,160},{160,192},{192,224},{1,3... | collective-permute-start | bytes 589832 | tf_op jit(solution)/shard_map/while/body/eval_jaxpr/ppermute | solution.py:12
  37.1 9.9 %collective-permute-start = (bf16[192,512]{1,0:T(8,128)(2,1)S(1)}, bf16[192,512]{1,0:T(8,128)(2,1)S(1)}, u32[]{:S(2)}, u32[]{:S(2)}) collective-permute-start(bf16[192,512]{1,0:T(8,128)(2,1)S(1)} %fusion.112), channel_id=1, source_target_pairs={{0,32},{32,64},{64,96},{96,128},{128,160},{160,192},{192,224},{1,3... | collective-permute-start | bytes 589832 | tf_op jit(solution)/shard_map/while/body/eval_jaxpr/ppermute | solution.py:12
  53.6 9.9 %collective-permute-start = (bf16[192,512]{1,0:T(8,128)(2,1)S(1)}, bf16[192,512]{1,0:T(8,128)(2,1)S(1)}, u32[]{:S(2)}, u32[]{:S(2)}) collective-permute-start(bf16[192,512]{1,0:T(8,128)(2,1)S(1)} %fusion.112), channel_id=1, source_target_pairs={{0,32},{32,64},{64,96},{96,128},{128,160},{160,192},{192,224},{1,3... | collective-permute-start | bytes 589832 | tf_op jit(solution)/shard_map/while/body/eval_jaxpr/ppermute | solution.py:12
  70.1 9.8 %collective-permute-start = (bf16[192,512]{1,0:T(8,128)(2,1)S(1)}, bf16[192,512]{1,0:T(8,128)(2,1)S(1)}, u32[]{:S(2)}, u32[]{:S(2)}) collective-permute-start(bf16[192,512]{1,0:T(8,128)(2,1)S(1)} %fusion.112), channel_id=1, source_target_pairs={{0,32},{32,64},{64,96},{96,128},{128,160},{160,192},{192,224},{1,3... | collective-permute-start | bytes 589832 | tf_op jit(solution)/shard_map/while/body/eval_jaxpr/ppermute | solution.py:12
  86.5 9.9 %collective-permute-start = (bf16[192,512]{1,0:T(8,128)(2,1)S(1)}, bf16[192,512]{1,0:T(8,128)(2,1)S(1)}, u32[]{:S(2)}, u32[]{:S(2)}) collective-permute-start(bf16[192,512]{1,0:T(8,128)(2,1)S(1)} %fusion.112), channel_id=1, source_target_pairs={{0,32},{32,64},{64,96},{96,128},{128,160},{160,192},{192,224},{1,3... | collective-permute-start | bytes 589832 | tf_op jit(solution)/shard_map/while/body/eval_jaxpr/ppermute | solution.py:12
  103.0 9.5 %collective-permute-start = (bf16[192,512]{1,0:T(8,128)(2,1)S(1)}, bf16[192,512]{1,0:T(8,128)(2,1)S(1)}, u32[]{:S(2)}, u32[]{:S(2)}) collective-permute-start(bf16[192,512]{1,0:T(8,128)(2,1)S(1)} %fusion.112), channel_id=1, source_target_pairs={{0,32},{32,64},{64,96},{96,128},{128,160},{160,192},{192,224},{1,3... | collective-permute-start | bytes 589832 | tf_op jit(solution)/shard_map/while/body/eval_jaxpr/ppermute | solution.py:12
  119.0 9.9 %collective-permute-start = (bf16[192,512]{1,0:T(8,128)(2,1)S(1)}, bf16[192,512]{1,0:T(8,128)(2,1)S(1)}, u32[]{:S(2)}, u32[]{:S(2)}) collective-permute-start(bf16[192,512]{1,0:T(8,128)(2,1)S(1)} %fusion.112), channel_id=1, source_target_pairs={{0,32},{32,64},{64,96},{96,128},{128,160},{160,192},{192,224},{1,3... | collective-permute-start | bytes 589832 | tf_op jit(solution)/shard_map/while/body/eval_jaxpr/ppermute | solution.py:12
  135.5 8.6 %collective-permute-start = (bf16[192,512]{1,0:T(8,128)(2,1)S(1)}, bf16[192,512]{1,0:T(8,128)(2,1)S(1)}, u32[]{:S(2)}, u32[]{:S(2)}) collective-permute-start(bf16[192,512]{1,0:T(8,128)(2,1)S(1)} %fusion.112), channel_id=1, source_target_pairs={{0,32},{32,64},{64,96},{96,128},{128,160},{160,192},{192,224},{1,3... | collective-permute-start | bytes 589832 | tf_op jit(solution)/shard_map/while/body/eval_jaxpr/ppermute | solution.py:12
  150.7 8.7 %collective-permute-start = (bf16[192,512]{1,0:T(8,128)(2,1)S(1)}, bf16[192,512]{1,0:T(8,128)(2,1)S(1)}, u32[]{:S(2)}, u32[]{:S(2)}) collective-permute-start(bf16[192,512]{1,0:T(8,128)(2,1)S(1)} %fusion.112), channel_id=1, source_target_pairs={{0,32},{32,64},{64,96},{96,128},{128,160},{160,192},{192,224},{1,3... | collective-permute-start | bytes 589832 | tf_op jit(solution)/shard_map/while/body/eval_jaxpr/ppermute | solution.py:12
  165.9 8.6 %collective-permute-start = (bf16[192,512]{1,0:T(8,128)(2,1)S(1)}, bf16[192,512]{1,0:T(8,128)(2,1)S(1)}, u32[]{:S(2)}, u32[]{:S(2)}) collective-permute-start(bf16[192,512]{1,0:T(8,128)(2,1)S(1)} %fusion.112), channel_id=1, source_target_pairs={{0,32},{32,64},{64,96},{96,128},{128,160},{160,192},{192,224},{1,3... | collective-permute-start | bytes 589832 | tf_op jit(solution)/shard_map/while/body/eval_jaxpr/ppermute | solution.py:12
  181.1 8.7 %collective-permute-start = (bf16[192,512]{1,0:T(8,128)(2,1)S(1)}, bf16[192,512]{1,0:T(8,128)(2,1)S(1)}, u32[]{:S(2)}, u32[]{:S(2)}) collective-permute-start(bf16[192,512]{1,0:T(8,128)(2,1)S(1)} %fusion.112), channel_id=1, source_target_pairs={{0,32},{32,64},{64,96},{96,128},{128,160},{160,192},{192,224},{1,3... | collective-permute-start | bytes 589832 | tf_op jit(solution)/shard_map/while/body/eval_jaxpr/ppermute | solution.py:12
  192.3 4.4 copy-start.1
  200.0 11.7 %collective-permute-start.1 = (bf16[192,512]{1,0:T(8,128)(2,1)}, bf16[192,512]{1,0:T(8,128)(2,1)S(1)}, u32[]{:S(2)}, u32[]{:S(2)}) collective-permute-start(bf16[192,512]{1,0:T(8,128)(2,1)} %fusion.134), channel_id=1, source_target_pairs={{32,0},{64,32},{96,64},{128,96},{160,128},{192,160},{224,192},{33,... | collective-permute-start | bytes 589832 | tf_op jit(solution)/shard_map/while/body/eval_jaxpr/ppermute | solution.py:12
  214.2 4.4 copy-start.1
  221.9 13.0 %collective-permute-start.1 = (bf16[192,512]{1,0:T(8,128)(2,1)}, bf16[192,512]{1,0:T(8,128)(2,1)S(1)}, u32[]{:S(2)}, u32[]{:S(2)}) collective-permute-start(bf16[192,512]{1,0:T(8,128)(2,1)} %fusion.134), channel_id=1, source_target_pairs={{32,0},{64,32},{96,64},{128,96},{160,128},{192,160},{224,192},{33,... | collective-permute-start | bytes 589832 | tf_op jit(solution)/shard_map/while/body/eval_jaxpr/ppermute | solution.py:12
  237.4 4.4 copy-start.1
  245.2 13.0 %collective-permute-start.1 = (bf16[192,512]{1,0:T(8,128)(2,1)}, bf16[192,512]{1,0:T(8,128)(2,1)S(1)}, u32[]{:S(2)}, u32[]{:S(2)}) collective-permute-start(bf16[192,512]{1,0:T(8,128)(2,1)} %fusion.134), channel_id=1, source_target_pairs={{32,0},{64,32},{96,64},{128,96},{160,128},{192,160},{224,192},{33,... | collective-permute-start | bytes 589832 | tf_op jit(solution)/shard_map/while/body/eval_jaxpr/ppermute | solution.py:12
  260.7 4.4 copy-start.1
  268.4 13.0 %collective-permute-start.1 = (bf16[192,512]{1,0:T(8,128)(2,1)}, bf16[192,512]{1,0:T(8,128)(2,1)S(1)}, u32[]{:S(2)}, u32[]{:S(2)}) collective-permute-start(bf16[192,512]{1,0:T(8,128)(2,1)} %fusion.134), channel_id=1, source_target_pairs={{32,0},{64,32},{96,64},{128,96},{160,128},{192,160},{224,192},{33,... | collective-permute-start | bytes 589832 | tf_op jit(solution)/shard_map/while/body/eval_jaxpr/ppermute | solution.py:12
  283.9 4.4 copy-start.1
  291.6 13.0 %collective-permute-start.1 = (bf16[192,512]{1,0:T(8,128)(2,1)}, bf16[192,512]{1,0:T(8,128)(2,1)S(1)}, u32[]{:S(2)}, u32[]{:S(2)}) collective-permute-start(bf16[192,512]{1,0:T(8,128)(2,1)} %fusion.134), channel_id=1, source_target_pairs={{32,0},{64,32},{96,64},{128,96},{160,128},{192,160},{224,192},{33,... | collective-permute-start | bytes 589832 | tf_op jit(solution)/shard_map/while/body/eval_jaxpr/ppermute | solution.py:12
  314.8 13.0 %collective-permute-start.1 = (bf16[192,512]{1,0:T(8,128)(2,1)}, bf16[192,512]{1,0:T(8,128)(2,1)S(1)}, u32[]{:S(2)}, u32[]{:S(2)}) collective-permute-start(bf16[192,512]{1,0:T(8,128)(2,1)} %fusion.134), channel_id=1, source_target_pairs={{32,0},{64,32},{96,64},{128,96},{160,128},{192,160},{224,192},{33,... | collective-permute-start | bytes 589832 | tf_op jit(solution)/shard_map/while/body/eval_jaxpr/ppermute | solution.py:12
  330.3 4.4 copy-start.1
  338.1 13.0 %collective-permute-start.1 = (bf16[192,512]{1,0:T(8,128)(2,1)}, bf16[192,512]{1,0:T(8,128)(2,1)S(1)}, u32[]{:S(2)}, u32[]{:S(2)}) collective-permute-start(bf16[192,512]{1,0:T(8,128)(2,1)} %fusion.134), channel_id=1, source_target_pairs={{32,0},{64,32},{96,64},{128,96},{160,128},{192,160},{224,192},{33,... | collective-permute-start | bytes 589832 | tf_op jit(solution)/shard_map/while/body/eval_jaxpr/ppermute | solution.py:12
  353.6 4.4 copy-start.1
  361.3 13.0 %collective-permute-start.1 = (bf16[192,512]{1,0:T(8,128)(2,1)}, bf16[192,512]{1,0:T(8,128)(2,1)S(1)}, u32[]{:S(2)}, u32[]{:S(2)}) collective-permute-start(bf16[192,512]{1,0:T(8,128)(2,1)} %fusion.134), channel_id=1, source_target_pairs={{32,0},{64,32},{96,64},{128,96},{160,128},{192,160},{224,192},{33,... | collective-permute-start | bytes 589832 | tf_op jit(solution)/shard_map/while/body/eval_jaxpr/ppermute | solution.py:12
  384.5 13.0 %collective-permute-start.1 = (bf16[192,512]{1,0:T(8,128)(2,1)}, bf16[192,512]{1,0:T(8,128)(2,1)S(1)}, u32[]{:S(2)}, u32[]{:S(2)}) collective-permute-start(bf16[192,512]{1,0:T(8,128)(2,1)} %fusion.134), channel_id=1, source_target_pairs={{32,0},{64,32},{96,64},{128,96},{160,128},{192,160},{224,192},{33,... | collective-permute-start | bytes 589832 | tf_op jit(solution)/shard_map/while/body/eval_jaxpr/ppermute | solution.py:12
  400.0 4.4 copy-start.1
  407.8 13.0 %collective-permute-start.1 = (bf16[192,512]{1,0:T(8,128)(2,1)}, bf16[192,512]{1,0:T(8,128)(2,1)S(1)}, u32[]{:S(2)}, u32[]{:S(2)}) collective-permute-start(bf16[192,512]{1,0:T(8,128)(2,1)} %fusion.134), channel_id=1, source_target_pairs={{32,0},{64,32},{96,64},{128,96},{160,128},{192,160},{224,192},{33,... | collective-permute-start | bytes 589832 | tf_op jit(solution)/shard_map/while/body/eval_jaxpr/ppermute | solution.py:12
  423.3 4.4 copy-start.1
  431.0 13.0 %collective-permute-start.1 = (bf16[192,512]{1,0:T(8,128)(2,1)}, bf16[192,512]{1,0:T(8,128)(2,1)S(1)}, u32[]{:S(2)}, u32[]{:S(2)}) collective-permute-start(bf16[192,512]{1,0:T(8,128)(2,1)} %fusion.134), channel_id=1, source_target_pairs={{32,0},{64,32},{96,64},{128,96},{160,128},{192,160},{224,192},{33,... | collective-permute-start | bytes 589832 | tf_op jit(solution)/shard_map/while/body/eval_jaxpr/ppermute | solution.py:12
  (14 other events, 53.9 us)
Sparse Core Ops, SparseCore 0:
  448.2 291.9 all-reduce.2
where the time goes:
time: 756 us; the launch traced here: 748 us
  waiting for transfers between devices  292 us (39%)
  matrix products  196 us (26%)
  other arithmetic  194 us (26%)
  starting transfers between devices  44.6 us (6%)
  between operations  14.1 us (2%)
    psum x1, waiting for transfers between devices, section_reduce(): lax.psum(total_in.astype(jnp.bfloat16), 'dp').astype(jnp.float32)  292 us
    dynamic_update_slice x33, other arithmetic, put_slot(): return lax.dynamic_update_index_in_dim(whole, chosen, slot_index, 0)  68.8 us
    add x11, other arithmetic, backward_step(): total_in = total_in + jnp.where(active, jnp.stack(grads_in), 0.0)  60.3 us
    ppermute x22, starting transfers between devices, passed_along(): lax.ppermute(value, axis, [(source, source + steps) for source in range(f...  44.5 us
    dot_general x22, matrix products, cell_backward(): grad_win = jnp.dot(normed.T, grad_pre, preferred_element_type=jnp.float32)  39 us
    dot_general x22, matrix products, cell_backward(): jnp.dot(grad_pre, weight_in.T, preferred_element_type=jnp.float32)  35.6 us
    dot_general x22, matrix products, cell_backward(): jnp.dot(grad_y, weight_out.T, preferred_element_type=jnp.float32)  33.1 us
    convert_element_type x22, other arithmetic, cell_backward(): (grad_y.astype(jnp.float32) + grad_wide).astype(jnp.bfloat16)  32 us
  transfers between devices with their start and end apart: 23, of which 1 were waited for; matrix products, arithmetic and copies ran while one was open for 27% of the time, Pallas kernels for 0%

commit v1 on v0

v1 whole, which is shorter than its diff:
```python
import jax
import jax.numpy as jnp
from jax import lax
from jax.experimental import pallas as pl
from jax.experimental.pallas import tpu as pltpu
from jax.sharding import PartitionSpec as P

norm_epsilon = 1e-06
f32, bf16 = jnp.float32, jnp.bfloat16
MESH = pl.DeviceIdType.MESH
C = 512
M = 4
R = 96
DMA = pltpu.SemaphoreType.DMA


def dot(a, b):
    return jnp.dot(a, b, preferred_element_type=f32)


def dot_bt(a, b):
    return lax.dot_general(a, b, (((1,), (1,)), ((), ())), preferred_element_type=f32)


def dot_at(a, b):
    return lax.dot_general(a, b, (((0,), (0,)), ((), ())), preferred_element_type=f32)


def kernel(
    img, og, wi, wo, gi_out, go_out,
    WI, WO, X, N, H, GP, GY, D, PRE, RS, G, RC, S, L1, L2, T, LZ,
    loc_w, loc_m, ag_s, ag_r, fw_s, fw_r, f_s, f_r, b_s, b_r, c_s, c_r, p_s, p_r, q_s, q_r, z_s, z_r,
):
    sec = lax.axis_index("section")
    dp = lax.axis_index("dp")
    y, xl = sec // 2, sec % 2
    xh, z, c = dp // 16, (dp // 2) % 8, dp % 2
    x = xh * 2 + xl

    def dev(x_, y_, z_, c_):
        return (y_ * 2 + x_ % 2, (x_ // 2) * 16 + z_ * 2 + c_)

    right, left = dev((x + 1) % 4, y, z, c), dev((x + 3) % 4, y, z, c)
    up, down = dev(x, (y + 1) % 4, z, c), dev(x, (y + 3) % 4, z, c)
    sib = dev(x, y, z, 1 - c)

    def ring_z(off):
        return dev(x, y, (z + off) % 8, c)

    def rc(src, dst, ss, rs, to):
        return pltpu.make_async_remote_copy(
            src_ref=src, dst_ref=dst, send_sem=ss, recv_sem=rs, device_id=to, device_id_type=MESH
        )

    mine, other = 2 * xl, 2 * (1 - xl)

    def load_w(i):
        src, dst = ((wi, WI), (wo, WO))[i]
        return pltpu.make_async_copy(src.at[0], dst.at[pl.ds(mine, 2)], loc_w.at[i])

    def load_img(m):
        return pltpu.make_async_copy(img.at[m, pl.ds(xl * R, R)], X.at[0, m], loc_m.at[m])

    def load_og(m):
        return pltpu.make_async_copy(og.at[m, pl.ds(xl * R, R)], GY.at[4, m], loc_m.at[m])

    load_w(0).start()
    load_w(1).start()

    @pl.when(y == 0)
    def _():
        for m in range(M):
            load_img(m).start()

    @pl.when(y == 3)
    def _():
        for m in range(M):
            load_og(m).start()

    bar = pltpu.get_barrier_semaphore()
    peers = [right, left, up, down, sib] + [ring_z(o) for o in range(1, 8)]
    for to in peers:
        pl.semaphore_signal(bar, inc=1, device_id=to, device_id_type=MESH)
    pl.semaphore_wait(bar, len(peers))

    def ag(t, side):
        src, dst = ((wi, WI), (wo, WO))[t % 2]
        k = t // 2
        rows = pl.ds(c * 256 + side * 128, 128)
        return rc(src.at[0, k, rows], dst.at[mine + k, rows], ag_s.at[t, side], ag_r.at[t, side], (right, left)[side])

    def fw(t):
        dst = (WI, WO)[t % 2]
        here = dst.at[other + t // 2, pl.ds(c * 256, 256)]
        return rc(here, here, fw_s.at[t], fw_r.at[t], sib)

    for t in range(4):
        for side in range(2):
            ag(t, side).start()
    for t in range(4):
        for side in range(2):
            ag(t, side).wait_recv()
        fw(t).start()
    load_w(0).wait()
    load_w(1).wait()
    for t in range(4):
        fw(t).wait_recv()

    def f_send(m):
        return rc(X.at[4, m], X.at[0, m], f_s.at[m], f_r.at[m], up)

    def forward(m, carry):
        @pl.when(y == 0)
        def _():
            load_img(m).wait()

        @pl.when(y > 0)
        def _():
            f_send(m).wait_recv()

        for j in range(4):
            xb = X[j, m]
            wide = xb.astype(f32)
            r = lax.rsqrt(jnp.mean(wide * wide, axis=-1, keepdims=True) + norm_epsilon)
            RS[j, m] = jnp.broadcast_to(r, (R, 128))
            N[j, m] = (wide * r).astype(bf16)
            p = dot(xb, WI[j]) * r
            PRE[j, m] = p
            s = 1.0 / (1.0 + jnp.exp(-p))
            h = p * s
            D[j, m] = s + h * (1.0 - s)
            hb = h.astype(bf16)
            H[j, m] = hb
            X[j + 1, m] = (wide + dot(hb, WO[j])).astype(bf16)

        @pl.when(y < 3)
        def _():
            f_send(m).start()

        return carry

    lax.fori_loop(0, M, forward, 0)

    def b_send(m):
        return rc(GY.at[0, m], GY.at[4, m], b_s.at[m], b_r.at[m], down)

    def backward(m, carry):
        @pl.when(y == 3)
        def _():
            load_og(m).wait()

        @pl.when(y < 3)
        def _():
            b_send(m).wait_recv()

        for j in range(3, -1, -1):
            gy = GY[j + 1, m]
            gp = (dot_bt(gy, WO[j]) * D[j, m]).astype(bf16)
            GP[j, m] = gp
            q = jnp.sum(gp.astype(f32) * PRE[j, m], axis=-1, keepdims=True) * (1.0 / C)
            gn = dot_bt(gp, WI[j])
            r = RS[j, m][:, :1]
            GY[j, m] = (gy.astype(f32) + r * (gn - N[j, m].astype(f32) * q)).astype(bf16)

        @pl.when(y > 0)
        def _():
            b_send(m).start()

        return carry

    lax.fori_loop(0, M, backward, 0)

    def cell_at(t):
        return lax.select(t < 2, mine + 1 - t, other + 3 - t)

    def c_send(t):
        j = cell_at(t)
        return rc(G.at[j, :, :, :, 1 - c], RC.at[j], c_s.at[t], c_r.at[t], sib)

    def weight(t, carry):
        j = cell_at(t)
        gi = dot_at(N[j].reshape(M * R, C), GP[j].reshape(M * R, C))
        G[j, 0] = gi.astype(bf16).reshape(2, 8, 2, 16, C)
        go = dot_at(H[j].reshape(M * R, C), GY[j + 1].reshape(M * R, C))
        G[j, 1] = go.astype(bf16).reshape(2, 8, 2, 16, C)
        c_send(t).start()
        return carry

    lax.fori_loop(0, 4, weight, 0)

    xh_r, xh_l = ((x + 1) % 4) // 2, ((x + 3) % 4) // 2

    def l1(k, side):
        return rc(
            S.at[mine + k, :, 1 - xh, pl.ds(side * 4, 4)], L1.at[k, side],
            p_s.at[k, side], p_r.at[k, side], (right, left)[side],
        )

    def l2(k, side, half):
        return rc(
            S.at[other + k, :, (xh_r, xh_l)[side], pl.ds(half * 4, 4)], L2.at[k, side, :, pl.ds(half * 4, 4)],
            q_s.at[k, side, half], q_r.at[k, side, half], (right, left)[side],
        )

    def sibling_sum(t):
        j = cell_at(t)
        c_send(t).wait_recv()
        S[j] = (G[j, :, :, :, c].astype(f32) + RC[j].astype(f32)).astype(bf16)

    def own_out(t, carry):
        sibling_sum(t)
        k = 1 - t
        l1(k, 0).start()
        l1(k, 1).start()
        return carry

    def other_out(t, carry):
        sibling_sum(t)
        k = 3 - t
        l2(k, 0, 1).start()
        l2(k, 1, 0).start()
        return carry

    lax.fori_loop(0, 2, own_out, 0)
    lax.fori_loop(2, 4, other_out, 0)

    def relay(t, carry):
        k = 1 - t
        for side, xd in ((0, xh_r), (1, xh_l)):
            l1(k, side).wait_recv()
            rows = pl.ds(side * 4, 4)
            S[other + k, :, xd, rows] = (
                S[other + k, :, xd, rows].astype(f32) + L1[k, side].astype(f32)
            ).astype(bf16)
            l2(k, side, side).start()
        return carry

    lax.fori_loop(0, 2, relay, 0)

    def z_send(k, off):
        return rc(T.at[k, :, (z + off) % 8], LZ.at[k, off - 1], z_s.at[k, off - 1], z_r.at[k, off - 1], ring_z(off))

    def collect(t, carry):
        k = 1 - t
        for side in range(2):
            for half in range(2):
                l2(k, side, half).wait_recv()
        T[k] = (S[mine + k, :, xh].astype(f32) + L2[k, 0].astype(f32) + L2[k, 1].astype(f32)).astype(bf16)
        for off in (4, 3, 5, 2, 6, 1, 7):
            z_send(k, off).start()
        return carry

    lax.fori_loop(0, 2, collect, 0)

    def finish(t, carry):
        k = 1 - t
        total = T[k, :, z].astype(f32)
        for off in range(1, 8):
            z_send(k, off).wait_recv()
            total = total + LZ[k, off - 1].astype(f32)
        gi_out[k] = total[0]
        go_out[k] = total[1]
        return carry

    lax.fori_loop(0, 2, finish, 0)

    for t in range(4):
        for side in range(2):
            ag(t, side).wait_send()
        fw(t).wait_send()
        c_send(jnp.int32(t)).wait_send()

    @pl.when(y < 3)
    def _():
        for m in range(M):
            f_send(m).wait_send()

    @pl.when(y > 0)
    def _():
        for m in range(M):
            b_send(m).wait_send()

    for k in range(2):
        for side in range(2):
            l1(k, side).wait_send()
            for half in range(2):
                l2(k, side, half).wait_send()
        for off in range(1, 8):
            z_send(k, off).wait_send()


def local(images, out_grad, w_in, w_out):
    V = pltpu.VMEM
    scratch = [
        V((4, C, C), bf16), V((4, C, C), bf16),
        V((5, M, R, C), bf16), V((4, M, R, C), bf16), V((4, M, R, C), bf16), V((4, M, R, C), bf16),
        V((5, M, R, C), bf16), V((4, M, R, C), f32), V((4, M, R, C), f32), V((4, M, R, 128), f32),
        V((4, 2, 2, 8, 2, 16, C), bf16), V((4, 2, 2, 8, 16, C), bf16), V((4, 2, 2, 8, 16, C), bf16),
        V((2, 2, 2, 4, 16, C), bf16), V((2, 2, 2, 8, 16, C), bf16), V((2, 2, 8, 16, C), bf16),
        V((2, 7, 2, 16, C), bf16),
        DMA((2,)), DMA((M,)), DMA((4, 2)), DMA((4, 2)), DMA((4,)), DMA((4,)),
        DMA((M,)), DMA((M,)), DMA((M,)), DMA((M,)), DMA((4,)), DMA((4,)),
        DMA((2, 2)), DMA((2, 2)), DMA((2, 2, 2)), DMA((2, 2, 2)), DMA((2, 7)), DMA((2, 7)),
    ]
    out = jax.ShapeDtypeStruct((2, 16, C), f32)
    grad_in, grad_out = pl.pallas_call(
        kernel,
        out_shape=(out, out),
        in_specs=[pl.BlockSpec(memory_space=pl.ANY)] * 4,
        out_specs=(pl.BlockSpec(memory_space=pltpu.VMEM),) * 2,
        scratch_shapes=scratch,
        compiler_params=pltpu.CompilerParams(
            collective_id=0, has_side_effects=True, vmem_limit_bytes=60 * 2**20
        ),
        name="window",
    )(images, out_grad, w_in, w_out)
    return grad_in[None], grad_out[None]


def solution(mesh):
    return jax.shard_map(
        local,
        mesh=mesh,
        in_specs=(
            P(None, "dp", None),
            P(None, "dp", None),
            P("section", None, None, None),
            P("section", None, None, None),
        ),
        out_specs=(P("section", None, "dp", None), P("section", None, "dp", None)),
        check_vma=False,
    )
```

time: 756 us -> 110 us (0.15)
  waiting for transfers between devices: 292 us -> 0 us
  matrix products: 196 us -> 0 us
  other arithmetic: 194 us -> 0 us
  Pallas kernels: 0 us -> 105 us
  starting transfers between devices: 44.6 us -> 0 us
  between operations: 14.1 us -> 0.65 us
    psum x1 -> x0, waiting for transfers between devices: 292 us -> none  [section_reduce(): lax.psum(total_in.astype(jnp.bfloat16), 'dp').astype(jnp.float32)]
    dot_general x132 -> x0, matrix products: 196 us -> none  [the longest x22 39 us: cell_backward(): grad_win = jnp.dot(normed.T, grad_pre, preferred_element_type=jnp.float32)]
    pallas_call x0 -> x1, Pallas kernels: none -> 105 us  [local(): pl.pallas_call(kernel, out_shape=(out, out), in_specs=[pl.BlockSpec(memor...]
    dynamic_update_slice x33 -> x0, other arithmetic: 68.8 us -> none  [put_slot(): return lax.dynamic_update_index_in_dim(whole, chosen, slot_index, 0)]
    add x11 -> x0, other arithmetic: 60.3 us -> none  [backward_step(): total_in = total_in + jnp.where(active, jnp.stack(grads_in), 0.0)]
    ppermute x22 -> x0, starting transfers between devices: 44.5 us -> none  [passed_along(): lax.ppermute(value, axis, [(source, source + steps) for source in range(f...]
    convert_element_type x24 -> x0, other arithmetic: 36 us -> none  [the longest x22 32 us: cell_backward(): (grad_y.astype(jnp.float32) + grad_wide).astype(jnp.bfloat16)]
    reduce_sum x11 -> x0, other arithmetic: 11.8 us -> none  [norm_scale(): jnp.mean(values * values, axis=-1, keepdims=True) + norm_epsilon]
  transfers between devices with their start and end apart: 23 -> 0, of which waited for: 1 -> 0; matrix products, arithmetic and copies ran while one was open for 27% -> 0% of each run, Pallas kernels for 0% -> 0%
where the time goes in v1:
time: 110 us; the launch traced here: 108 us
  Pallas kernels  105 us (95%)
  local copies, waits for them, and re-layouts  2.14 us (2%)
    pallas_call x1, Pallas kernels, local(): pl.pallas_call(kernel, out_shape=(out, out), in_specs=[pl.BlockSpec(memor...  105 us

profile of v1, /device:TPU:1, one launch (start us, length us, event | category | flops | bytes accessed | tf_op | source)
XLA Modules:
  0.0 108.1 jit_solution(9446311976389432166)
XLA Ops:
  0.6 105.3 %window.1 = (f32[2,16,512]{2,1,0:T(8,128)}, f32[2,16,512]{2,1,0:T(8,128)}) custom-call(bf16[4,192,512]{2,1,0:T(8,128)(2,1)} %img.1, bf16[4,192,512]{2,1,0:T(8,128)(2,1)} %og.1, bf16[1,2,512,512]{3,2,1,0:T(8,128)(2,1)} %wi.1, bf16[1,2,512,512]{3,2,1,0:T(8,128)(2,1)} %wo.1), custom_call_target="tpu_custom_call" | custom-call | tf_op jit(solution)/shard_map/window/pallas_call | solution.py:306
  105.9 0.0 copy-start
  105.9 1.5 %copy.8 = f32[1,2,16,512]{3,2,1,0:T(8,128)} copy(f32[1,2,16,512]{3,2,1,0:T(8,128)} %bitcast.3) | data formatting | bytes 131072
  107.4 0.0 copy-done
  107.4 0.6 copy.9
Async XLA Ops:
  105.9 1.5 %copy-start = (f32[2,16,512]{2,1,0:T(8,128)S(1)}, f32[2,16,512]{2,1,0:T(8,128)}, u32[]{:S(2)}) copy-start(f32[2,16,512]{2,1,0:T(8,128)} %get-tuple-element.5) | copy-start | bytes 196612

commit v2 on v1

v2 whole, which is shorter than its diff:
```python
import jax
import jax.numpy as jnp
from jax import lax
from jax.experimental import pallas as pl
from jax.experimental.pallas import tpu as pltpu
from jax.sharding import PartitionSpec as P

norm_epsilon = 1e-06
f32, bf16 = jnp.float32, jnp.bfloat16
MESH = pl.DeviceIdType.MESH
C = 512
M = 4
R = 96
DMA = pltpu.SemaphoreType.DMA


def dot(a, b):
    return jnp.dot(a, b, preferred_element_type=f32)


def dot_at(a, b):
    return lax.dot_general(a, b, (((0,), (0,)), ((), ())), preferred_element_type=f32)


def kernel(
    img, og, wi, wo, gi_out, go_out,
    WI, WO, WIT, WOT, X, XT, XO, N, H, GP, GY, D, PRE, RS, G, RC, S, L1, L2, T, LZ,
    loc_w, loc_m, loc_x, ag_s, ag_r, fw_s, fw_r, g_s, g_r, f_s, f_r, b_s, b_r, c_s, c_r, p_s, p_r, q_s, q_r, z_s, z_r,
    near_z, diag,
):
    sec = lax.axis_index("section")
    dp = lax.axis_index("dp")
    y, xl = sec // 2, sec % 2
    xh, z, c = dp // 16, (dp // 2) % 8, dp % 2
    x = xh * 2 + xl

    def dev(x_, y_, z_, c_):
        return (y_ * 2 + x_ % 2, (x_ // 2) * 16 + z_ * 2 + c_)

    right, left = dev((x + 1) % 4, y, z, c), dev((x + 3) % 4, y, z, c)
    up, down = dev(x, (y + 1) % 4, z, c), dev(x, (y + 3) % 4, z, c)
    up_right = dev((x + 1) % 4, (y + 1) % 4, z, c)
    sib = dev(x, y, z, 1 - c)

    def ring_z(off):
        return dev(x, y, (z + off) % 8, c)

    def rc(src, dst, ss, rs, to):
        return pltpu.make_async_remote_copy(
            src_ref=src, dst_ref=dst, send_sem=ss, recv_sem=rs, device_id=to, device_id_type=MESH
        )

    def signal(sem, to):
        pl.semaphore_signal(sem, inc=1, device_id=to, device_id_type=MESH)

    mine, other = 2 * xl, 2 * (1 - xl)

    def load_w(i):
        src, dst = ((wi, WI), (wo, WO))[i]
        return pltpu.make_async_copy(src.at[0], dst.at[pl.ds(mine, 2)], loc_w.at[i])

    def load_img(m):
        return pltpu.make_async_copy(img.at[m, pl.ds(xl * R, R)], X.at[0, m], loc_m.at[m])

    def load_partner_img(m):
        return pltpu.make_async_copy(img.at[m, pl.ds(R, R)], XT.at[m], loc_x.at[m])

    def load_og(m):
        return pltpu.make_async_copy(og.at[m, pl.ds(xl * R, R)], GY.at[4, m], loc_m.at[m])

    load_w(0).start()
    load_w(1).start()

    @pl.when(y == 0)
    def _():
        for m in range(M):
            load_img(m).start()

            @pl.when(xl == 0)
            def _():
                load_partner_img(m).start()

    @pl.when(y == 3)
    def _():
        for m in range(M):
            load_og(m).start()

    bar = pltpu.get_barrier_semaphore()
    peers = [right, left, up, down, sib, ring_z(1), ring_z(7)]
    for to in peers:
        signal(bar, to)
    pl.semaphore_wait(bar, len(peers))

    def z_round(n):
        for off in (1, 7):
            signal(near_z.at[n], ring_z(off))

    z_round(0)

    @pl.when((y == 1) & (xl == 1))
    def _():
        signal(diag, down)

    def ag(t, side):
        src, dst = ((wi, WI), (wo, WO))[t % 2]
        k = t // 2
        rows = pl.ds(c * 256 + side * 128, 128)
        return rc(src.at[0, k, rows], dst.at[mine + k, rows], ag_s.at[t, side], ag_r.at[t, side], (right, left)[side])

    def ag_start():
        for t in range(4):
            for side in range(2):
                ag(t, side).start()

    def fw(t):
        dst = (WI, WO)[t % 2]
        here = dst.at[other + t // 2, pl.ds(c * 256, 256)]
        return rc(here, here, fw_s.at[t], fw_r.at[t], sib)

    def ag_forward():
        for t in range(4):
            for side in range(2):
                ag(t, side).wait_recv()
            fw(t).start()

    def fw_wait():
        for t in range(4):
            fw(t).wait_recv()

    def transpose_weights():
        def one(j, carry):
            WIT[j] = WI[j].T
            WOT[j] = WO[j].T
            return carry

        lax.fori_loop(0, 4, one, 0)

    def cell(xb, j, m, save=True, finish=True):
        wide = xb.astype(f32)
        r = lax.rsqrt(jnp.mean(wide * wide, axis=-1, keepdims=True) + norm_epsilon)
        p = dot(xb, WI[j]) * r
        s = 1.0 / (1.0 + jnp.exp(-p))
        h = p * s
        hb = h.astype(bf16)
        if save:
            RS[j, m] = jnp.broadcast_to(r, (R, 128))
            N[j, m] = (wide * r).astype(bf16)
            PRE[j, m] = p
            D[j, m] = s + h * (1.0 - s)
            H[j, m] = hb
        if finish:
            return (wide + dot(hb, WO[j])).astype(bf16)

    def f_send(m):
        return rc(X.at[4, m], X.at[0, m], f_s.at[m], f_r.at[m], up)

    def to_left(m):
        return rc(X.at[2, m], XT.at[m], g_s.at[m, 0], g_r.at[m, 1], left)

    def to_right(m):
        return rc(XO.at[m], X.at[2, m], g_s.at[m, 1], g_r.at[m, 0], right)

    def to_up(m):
        return rc(X.at[4, m], X.at[0, m], g_s.at[m, 0], f_r.at[m], up)

    def to_up_right(m):
        return rc(XO.at[m], X.at[0, m], g_s.at[m, 1], f_r.at[m], up_right)

    def first_row(m, carry):
        @pl.when(xl == 0)
        def _():
            load_img(m).wait()

        @pl.when(xl == 1)
        def _():
            to_right(m).wait_recv()

        xb = X[mine, m]
        for i in range(2):
            xb = cell(xb, mine + i, m)
            X[mine + i + 1, m] = xb

        @pl.when(xl == 0)
        def _():
            to_left(m).start()
            load_partner_img(m).wait()

        @pl.when(xl == 1)
        def _():
            to_up(m).start()
            to_left(m).wait_recv()

        xb = XT[m]
        for i in range(2):
            xb = cell(xb, mine + i, m, save=False)
        XO[m] = xb

        @pl.when(xl == 0)
        def _():
            to_right(m).start()

        @pl.when(xl == 1)
        def _():
            to_up_right(m).start()

        return carry

    def again(m, carry):
        X[other + 1, m] = cell(X[other, m], other, m)
        cell(X[other + 1, m], other + 1, m, finish=False)
        return carry

    def forward(m, carry):
        f_send(m).wait_recv()
        for j in range(4):
            for i in range(2):
                @pl.when((m == 0) & (y == 1) & (xl != j // 2))
                def _():
                    fw(2 * (j % 2) + i).wait_recv()

            X[j + 1, m] = cell(X[j, m], j, m)

        @pl.when(y < 3)
        def _():
            f_send(m).start()

        return carry

    @pl.when((y > 0) | (xl == 1))
    def _():
        ag_start()

    load_w(0).wait()
    load_w(1).wait()

    @pl.when(y == 0)
    def _():
        @pl.when(xl == 1)
        def _():
            pl.semaphore_wait(diag, 1)

        lax.fori_loop(0, M, first_row, 0)

        @pl.when(xl == 0)
        def _():
            ag_start()

        ag_forward()
        fw_wait()

        @pl.when(xl == 1)
        def _():
            for m in range(M):
                load_img(m).wait()

        lax.fori_loop(0, M, again, 0)

    @pl.when(y > 0)
    def _():
        ag_forward()

        @pl.when(y > 1)
        def _():
            fw_wait()
            transpose_weights()

        lax.fori_loop(0, M, forward, 0)

    @pl.when(y < 2)
    def _():
        transpose_weights()

    pl.semaphore_wait(near_z.at[0], 2)
    z_round(1)

    def b_send(m):
        return rc(GY.at[0, m], GY.at[4, m], b_s.at[m], b_r.at[m], down)

    def backward(m, carry):
        @pl.when(y == 3)
        def _():
            load_og(m).wait()

        @pl.when(y < 3)
        def _():
            b_send(m).wait_recv()

        for j in range(3, -1, -1):
            gy = GY[j + 1, m]
            gp = (dot(gy, WOT[j]) * D[j, m]).astype(bf16)
            GP[j, m] = gp
            q = jnp.sum(gp.astype(f32) * PRE[j, m], axis=-1, keepdims=True) * (1.0 / C)
            gn = dot(gp, WIT[j])
            r = RS[j, m][:, :1]
            GY[j, m] = (gy.astype(f32) + r * (gn - N[j, m].astype(f32) * q)).astype(bf16)

        @pl.when(y > 0)
        def _():
            b_send(m).start()

        return carry

    lax.fori_loop(0, 2, backward, 0)
    pl.semaphore_wait(near_z.at[1], 2)
    z_round(2)
    lax.fori_loop(2, M, backward, 0)

    def c_send(j, io):
        return rc(G.at[j, io, :, :, 1 - c], RC.at[j, io], c_s.at[j, io], c_r.at[j, io], sib)

    def weight(j, io):
        a, b = ((N.at[j], GP.at[j]), (H.at[j], GY.at[j + 1]))[io]
        g = dot_at(a[...].reshape(M * R, C), b[...].reshape(M * R, C))
        G[j, io] = g.astype(bf16).reshape(2, 8, 2, 16, C)
        c_send(j, io).start()

    xh_r, xh_l = ((x + 1) % 4) // 2, ((x + 3) % 4) // 2

    def l1(k, io, side):
        return rc(
            S.at[mine + k, io, 1 - xh, pl.ds(side * 4, 4)], L1.at[k, io, side],
            p_s.at[k, io, side], p_r.at[k, io, side], (right, left)[side],
        )

    def l2(k, io, side, half):
        rows = pl.ds(half * 4, 4)
        return rc(
            S.at[other + k, io, (xh_r, xh_l)[side], rows], L2.at[k, io, side, rows],
            q_s.at[k, io, side, half], q_r.at[k, io, side, half], (right, left)[side],
        )

    def sibling_sum(j, io):
        c_send(j, io).wait_recv()
        S[j, io] = (G[j, io, :, :, c].astype(f32) + RC[j, io].astype(f32)).astype(bf16)

    pieces = [(1, 0), (1, 1), (0, 0), (0, 1)]

    def own_out(k, io):
        sibling_sum(mine + k, io)
        l1(k, io, 0).start()
        l1(k, io, 1).start()

    for k, io in pieces:
        weight(mine + k, io)
    for n in range(4):
        weight(other + pieces[n][0], pieces[n][1])
        own_out(*pieces[n])

    for k, io in pieces:
        sibling_sum(other + k, io)
        l2(k, io, 0, 1).start()
        l2(k, io, 1, 0).start()
        for side, xd in ((0, xh_r), (1, xh_l)):
            l1(k, io, side).wait_recv()
            rows = pl.ds(side * 4, 4)
            S[other + k, io, xd, rows] = (
                S[other + k, io, xd, rows].astype(f32) + L1[k, io, side].astype(f32)
            ).astype(bf16)
            l2(k, io, side, side).start()

    pl.semaphore_wait(near_z.at[2], 2)

    def z_send(k, io, off):
        return rc(
            T.at[k, io, (z + off) % 8], LZ.at[k, io, off - 1],
            z_s.at[k, io, off - 1], z_r.at[k, io, off - 1], ring_z(off),
        )

    for k, io in pieces:
        for side in range(2):
            for half in range(2):
                l2(k, io, side, half).wait_recv()
        T[k, io] = (
            S[mine + k, io, xh].astype(f32) + L2[k, io, 0].astype(f32) + L2[k, io, 1].astype(f32)
        ).astype(bf16)
        for off in (4, 3, 5, 2, 6, 1, 7):
            z_send(k, io, off).start()

    for k, io in pieces:
        total = T[k, io, z].astype(f32)
        for off in range(1, 8):
            z_send(k, io, off).wait_recv()
            total = total + LZ[k, io, off - 1].astype(f32)
        (gi_out, go_out)[io][k] = total

    for t in range(4):
        for side in range(2):
            ag(t, side).wait_send()
        fw(t).wait_send()

    @pl.when(y == 0)
    def _():
        for m in range(M):
            to_left(m).wait_send()
            to_right(m).wait_send()

    @pl.when((y > 0) & (y < 3))
    def _():
        for m in range(M):
            f_send(m).wait_send()

    @pl.when(y > 0)
    def _():
        for m in range(M):
            b_send(m).wait_send()

    for j in range(4):
        for io in range(2):
            c_send(j, io).wait_send()
    for k, io in pieces:
        for side in range(2):
            l1(k, io, side).wait_send()
            for half in range(2):
                l2(k, io, side, half).wait_send()
        for off in range(1, 8):
            z_send(k, io, off).wait_send()


def local(images, out_grad, w_in, w_out):
    V = pltpu.VMEM
    REG = pltpu.SemaphoreType.REGULAR
    weights = V((4, C, C), bf16)
    acts = V((4, M, R, C), bf16)
    wide = V((4, M, R, C), f32)
    scratch = [
        weights, weights, weights, weights,
        V((5, M, R, C), bf16), V((M, R, C), bf16), V((M, R, C), bf16),
        acts, acts, acts, V((5, M, R, C), bf16), wide, wide, V((4, M, R, 128), f32),
        V((4, 2, 2, 8, 2, 16, C), bf16), V((4, 2, 2, 8, 16, C), bf16), V((4, 2, 2, 8, 16, C), bf16),
        V((2, 2, 2, 4, 16, C), bf16), V((2, 2, 2, 8, 16, C), bf16), V((2, 2, 8, 16, C), bf16),
        V((2, 2, 7, 16, C), bf16),
        DMA((2,)), DMA((M,)), DMA((M,)), DMA((4, 2)), DMA((4, 2)), DMA((4,)), DMA((4,)),
        DMA((M, 2)), DMA((M, 2)), DMA((M,)), DMA((M,)), DMA((M,)), DMA((M,)), DMA((4, 2)), DMA((4, 2)),
        DMA((2, 2, 2)), DMA((2, 2, 2)), DMA((2, 2, 2, 2)), DMA((2, 2, 2, 2)), DMA((2, 2, 7)), DMA((2, 2, 7)),
        REG((3,)), REG,
    ]
    out = jax.ShapeDtypeStruct((2, 16, C), f32)
    grad_in, grad_out = pl.pallas_call(
        kernel,
        out_shape=(out, out),
        in_specs=[pl.BlockSpec(memory_space=pl.ANY)] * 4,
        out_specs=(pl.BlockSpec(memory_space=pltpu.VMEM),) * 2,
        scratch_shapes=scratch,
        compiler_params=pltpu.CompilerParams(
            collective_id=0, has_side_effects=True, vmem_limit_bytes=60 * 2**20
        ),
        name="window",
    )(images, out_grad, w_in, w_out)
    return grad_in[None], grad_out[None]


def solution(mesh):
    return jax.shard_map(
        local,
        mesh=mesh,
        in_specs=(
            P(None, "dp", None),
            P(None, "dp", None),
            P("section", None, None, None),
            P("section", None, None, None),
        ),
        out_specs=(P("section", None, "dp", None), P("section", None, "dp", None)),
        check_vma=False,
    )
```

time: 110 us -> 100 us (0.909)
  Pallas kernels: 105 us -> 96.1 us
    pallas_call x1, Pallas kernels: 105 us -> 96.1 us  [local(): pl.pallas_call(kernel, out_shape=(out, out), in_specs=[pl.BlockSpec(memor...]
where the time goes in v2:
time: 100 us; the launch traced here: 98.9 us
  Pallas kernels  96.1 us (96%)
  local copies, waits for them, and re-layouts  2.14 us (2%)
    pallas_call x1, Pallas kernels, local(): pl.pallas_call(kernel, out_shape=(out, out), in_specs=[pl.BlockSpec(memor...  96.1 us
    unnamed x4, local copies, waits for them, and re-layouts  2.14 us

profile of v2, /device:TPU:1, one launch (start us, length us, event | category | flops | bytes accessed | tf_op | source)
XLA Modules:
  0.0 98.9 jit_solution(3823815073675320304)
XLA Ops:
  0.6 96.1 %window.1 = (f32[2,16,512]{2,1,0:T(8,128)}, f32[2,16,512]{2,1,0:T(8,128)}) custom-call(bf16[4,192,512]{2,1,0:T(8,128)(2,1)} %img.1, bf16[4,192,512]{2,1,0:T(8,128)(2,1)} %og.1, bf16[1,2,512,512]{3,2,1,0:T(8,128)(2,1)} %wi.1, bf16[1,2,512,512]{3,2,1,0:T(8,128)(2,1)} %wo.1), custom_call_target="tpu_custom_call" | custom-call | tf_op jit(solution)/shard_map/window/pallas_call | solution.py:438
  96.7 0.0 copy-start
  96.7 1.5 %copy.8 = f32[1,2,16,512]{3,2,1,0:T(8,128)} copy(f32[1,2,16,512]{3,2,1,0:T(8,128)} %bitcast.3) | data formatting | bytes 131072
  98.3 0.0 copy-done
  98.3 0.6 copy.9
Async XLA Ops:
  96.7 1.5 %copy-start = (f32[2,16,512]{2,1,0:T(8,128)S(1)}, f32[2,16,512]{2,1,0:T(8,128)}, u32[]{:S(2)}) copy-start(f32[2,16,512]{2,1,0:T(8,128)} %get-tuple-element.5) | copy-start | bytes 196612

commit v3 on v2

v3 whole, which is shorter than its diff:
```python
import jax
import jax.numpy as jnp
from jax import lax
from jax.experimental import pallas as pl
from jax.experimental.pallas import tpu as pltpu
from jax.sharding import PartitionSpec as P

norm_epsilon = 1e-06
f32, bf16 = jnp.float32, jnp.bfloat16
MESH = pl.DeviceIdType.MESH
C = 512
M = 4
R = 96
BATCH = 2
OWN = M * R
UNIT = 96 if R % 96 == 0 else (48 if R == 48 else 32)
UNITS = OWN // UNIT
SHARED, PLAIN = (1, 2, 3), (0,)
DMA = pltpu.SemaphoreType.DMA


def dot(a, b):
    return jnp.dot(a, b, preferred_element_type=f32)


def dot_at(a, b):
    return lax.dot_general(a, b, (((0,), (0,)), ((), ())), preferred_element_type=f32)


def kernel(
    img, og, wi, wo, gi_out, go_out,
    WI, WO, WIT, WOT, X, XT, XO, N, H, GP, GY, D, PRE, RS, G, L1, L2, T, LZ,
    loc_w, loc_m, loc_x, ag_s, ag_r, fw_s, fw_r, zf_s, zf_r, g_s, g_r, f_s, f_r, b_s, b_r, n_s, n_r, e_s, e_r, p_s, p_r, q_s, q_r, z_s, z_r,
    near_z, diag,
):
    sec = lax.axis_index("section")
    dp = lax.axis_index("dp")
    y, xl = sec // 2, sec % 2
    xh, z, c = dp // 16, (dp // 2) % 8, dp % 2
    x = xh * 2 + xl

    def dev(x_, y_, z_, c_):
        return (y_ * 2 + x_ % 2, (x_ // 2) * 16 + z_ * 2 + c_)

    right, left = dev((x + 1) % 4, y, z, c), dev((x + 3) % 4, y, z, c)
    up, down = dev(x, (y + 1) % 4, z, c), dev(x, (y + 3) % 4, z, c)
    up_right = dev((x + 1) % 4, (y + 1) % 4, z, c)
    sib = dev(x, y, z, 1 - c)

    def ring_z(off):
        return dev(x, y, (z + off) % 8, c)

    def rc(src, dst, ss, rs, to):
        return pltpu.make_async_remote_copy(
            src_ref=src, dst_ref=dst, send_sem=ss, recv_sem=rs, device_id=to, device_id_type=MESH
        )

    def signal(sem, to):
        pl.semaphore_signal(sem, inc=1, device_id=to, device_id_type=MESH)

    mine, other = 2 * xl, 2 * (1 - xl)

    def load_w(i):
        src, dst = ((wi, WI), (wo, WO))[i]
        return pltpu.make_async_copy(src.at[0], dst.at[pl.ds(mine, 2)], loc_w.at[i])

    def load_rows(i, src, half, dst, sem):
        per = 96 // UNIT
        rows = src.at[i // per, pl.ds(half * 96 + (i % per) * UNIT, UNIT)]
        return pltpu.make_async_copy(rows, dst.at[i * UNIT // R, pl.ds(i * UNIT % R, UNIT)], sem.at[i])

    def load_img(i):
        return load_rows(i, img, xl, X.at[0], loc_m)

    def load_partner_img(i):
        return load_rows(i, img, 1, XT, loc_x)

    def load_og(i):
        return load_rows(i, og, xl, GY.at[4, 0], loc_m)

    load_w(0).start()
    load_w(1).start()

    @pl.when(y == 0)
    def _():
        for i in range(UNITS):
            load_img(i).start()

        @pl.when(xl == 0)
        def _():
            for i in range(UNITS):
                load_partner_img(i).start()

    @pl.when(y == 3)
    def _():
        for i in range(UNITS):
            load_og(i).start()

    bar = pltpu.get_barrier_semaphore()
    peers = [right, left, up, down, sib, ring_z(1), ring_z(7)]
    for to in peers:
        signal(bar, to)
    pl.semaphore_wait(bar, len(peers))

    def z_round(n):
        for off in (1, 7):
            signal(near_z.at[n], ring_z(off))

    z_round(0)

    @pl.when((y == 1) & (xl == 1))
    def _():
        signal(diag, down)

    def ag(t, side):
        src, dst = ((wi, WI), (wo, WO))[t % 2]
        k = t // 2
        if t in SHARED:
            rows = pl.ds(c * 256 + side * 128 + (z % 2) * 64, 64)
        else:
            rows = pl.ds(c * 256 + side * 128, 128)
        return rc(src.at[0, k, rows], dst.at[mine + k, rows], ag_s.at[t, side], ag_r.at[t, side], (right, left)[side])

    def ag_start():
        for t in SHARED + PLAIN:
            for side in range(2):
                ag(t, side).start()

    def zf(t, side):
        here = (WI, WO)[t % 2].at[other + t // 2, pl.ds(c * 256 + side * 128 + (z % 2) * 64, 64)]
        return rc(here, here, zf_s.at[t, side], zf_r.at[t, side], ring_z((1, 7)[side]))

    def fw(t):
        dst = (WI, WO)[t % 2]
        here = dst.at[other + t // 2, pl.ds(c * 256, 256)]
        return rc(here, here, fw_s.at[t], fw_r.at[t], sib)

    def ag_forward():
        for t in SHARED:
            for side in range(2):
                ag(t, side).wait_recv()
                zf(t, side).start()
        for t in PLAIN:
            for side in range(2):
                ag(t, side).wait_recv()
            fw(t).start()
        for t in SHARED:
            for side in range(2):
                zf(t, side).wait_recv()
            fw(t).start()

    def fw_wait():
        for t in range(4):
            fw(t).wait_recv()

    def transpose_weights():
        def one(j, carry):
            WIT[j] = WI[j].T
            WOT[j] = WO[j].T
            return carry

        lax.fori_loop(0, 4, one, 0)

    def put(ref, j, ms, value):
        if isinstance(ms, pl.Slice):
            value = value.reshape(ms.size, R, value.shape[-1])
        ref[j, ms] = value

    def put_own(ref, j, ms, value):
        if isinstance(ms, pl.Slice):
            value = value.reshape(ms.size, R, value.shape[-1])
        ref[j, 0, ms] = value

    def flat(value):
        return value.reshape(-1, value.shape[-1])

    def cell(xb, j, ms, save=True, finish=True):
        wide = xb.astype(f32)
        r = lax.rsqrt(jnp.mean(wide * wide, axis=-1, keepdims=True) + norm_epsilon)
        p = dot(xb, WI[j]) * r
        s = 1.0 / (1.0 + jnp.exp(-p))
        h = p * s
        hb = h.astype(bf16)
        if save:
            put(RS, j, ms, jnp.broadcast_to(r, (r.shape[0], 128)))
            put_own(N, j, ms, (wide * r).astype(bf16))
            put(PRE, j, ms, p)
            put(D, j, ms, s + h * (1.0 - s))
            put_own(H, j, ms, hb)
        if finish:
            return (wide + dot(hb, WO[j])).astype(bf16)

    def f_send(m):
        return rc(X.at[4, m], X.at[0, m], f_s.at[m], f_r.at[m], up)

    def to_left(m):
        return rc(X.at[2, m], XT.at[m], g_s.at[m, 0], g_r.at[m, 1], left)

    def to_right(m):
        return rc(XO.at[m], X.at[2, m], g_s.at[m, 1], g_r.at[m, 0], right)

    def to_up(m):
        return rc(X.at[4, m], X.at[0, m], g_s.at[m, 0], f_r.at[m], up)

    def to_up_right(m):
        return rc(XO.at[m], X.at[0, m], g_s.at[m, 1], f_r.at[m], up_right)

    def first_row(m, carry):
        @pl.when(xl == 1)
        def _():
            to_right(m).wait_recv()

        xb = X[mine, m]
        for i in range(2):
            xb = cell(xb, mine + i, m)
            X[mine + i + 1, m] = xb

        @pl.when(xl == 0)
        def _():
            to_left(m).start()

        @pl.when(xl == 1)
        def _():
            to_up(m).start()
            to_left(m).wait_recv()

        xb = XT[m]
        for i in range(2):
            xb = cell(xb, mine + i, m, save=False)
        XO[m] = xb

        @pl.when(xl == 0)
        def _():
            to_right(m).start()

        @pl.when(xl == 1)
        def _():
            to_up_right(m).start()

        return carry

    def again(m, carry):
        X[other + 1, m] = cell(X[other, m], other, m)
        cell(X[other + 1, m], other + 1, m, finish=False)
        return carry

    def forward(m, carry):
        f_send(m).wait_recv()
        for j in range(4):
            for i in range(2):
                @pl.when((m == 0) & (y == 1) & (xl != j // 2))
                def _():
                    fw(2 * (j % 2) + i).wait_recv()

            X[j + 1, m] = cell(X[j, m], j, m)

        f_send(m).start()
        return carry

    def b_send(m):
        return rc(GY.at[0, 0, m], GY.at[4, 0, m], b_s.at[m], b_r.at[m], down)

    def nh_send(i, io):
        ref, j = (N, H)[io], 2 * i + 1 - c
        return rc(ref.at[j, 0], ref.at[j, 1], n_s.at[i, io], n_r.at[i, io], sib)

    def e_send(i, io, m):
        ref, j = (GP, GY)[io], 2 * i + 1 - c + io
        return rc(ref.at[j, 0, m], ref.at[j, 1, m], e_s.at[i, io, m], e_r.at[i, io, m], sib)

    def cells_back(ms, mlist):
        for j in range(3, -1, -1):
            gy = flat(GY[j + 1, 0, ms])
            gp = (dot(gy, WOT[j]) * flat(D[j, ms])).astype(bf16)
            put_own(GP, j, ms, gp)
            q = jnp.sum(gp.astype(f32) * flat(PRE[j, ms]), axis=-1, keepdims=True) * (1.0 / C)
            gn = dot(gp, WIT[j])
            r = flat(RS[j, ms])[:, :1]
            n = flat(N[j, 0, ms]).astype(f32)
            put_own(GY, j, ms, (gy.astype(f32) + r * (gn - n * q)).astype(bf16))

            @pl.when(c != j % 2)
            def _():
                for m in mlist:
                    e_send(j // 2, 0, m).start()
                    e_send(j // 2, 1, m).start()

    def backward(m, carry):
        b_send(m).wait_recv()
        cells_back(m, [m])

        @pl.when(y > 0)
        def _():
            b_send(m).start()

        return carry

    def last_row(g, carry):
        mlist = [g * BATCH + i for i in range(BATCH)]
        ms = pl.ds(g * BATCH, BATCH)
        for m in mlist:
            f_send(m).wait_recv()
        xb = flat(X[0, ms])
        for j in range(4):
            xb = cell(xb, j, ms, finish=j < 3)
        cells_back(ms, mlist)
        for m in mlist:
            b_send(m).start()
        return carry

    @pl.when((y > 0) | (xl == 1))
    def _():
        ag_start()

    load_w(0).wait()
    load_w(1).wait()

    @pl.when(y == 0)
    def _():
        @pl.when(xl == 1)
        def _():
            pl.semaphore_wait(diag, 1)

        @pl.when(xl == 0)
        def _():
            for i in range(UNITS):
                load_img(i).wait()
                load_partner_img(i).wait()

        lax.fori_loop(0, M, first_row, 0)

        @pl.when(xl == 0)
        def _():
            ag_start()

        ag_forward()
        fw_wait()

        @pl.when(xl == 1)
        def _():
            for i in range(UNITS):
                load_img(i).wait()

        lax.fori_loop(0, M, again, 0)

    @pl.when(y > 0)
    def _():
        ag_forward()

        @pl.when(y > 1)
        def _():
            fw_wait()
            transpose_weights()

        @pl.when(y < 3)
        def _():
            lax.fori_loop(0, M, forward, 0)

        @pl.when(y == 3)
        def _():
            for i in range(UNITS):
                load_og(i).wait()
            lax.fori_loop(0, M // BATCH, last_row, 0)

    @pl.when(y < 2)
    def _():
        transpose_weights()

    for i in range(2):
        for io in range(2):
            nh_send(i, io).start()
    pl.semaphore_wait(near_z.at[0], 2)
    z_round(1)

    @pl.when(y < 3)
    def _():
        lax.fori_loop(0, 1, backward, 0)

    pl.semaphore_wait(near_z.at[1], 2)
    z_round(2)

    @pl.when(y < 3)
    def _():
        lax.fori_loop(1, 2, backward, 0)

    pl.semaphore_wait(near_z.at[2], 2)
    z_round(3)

    @pl.when(y < 3)
    def _():
        lax.fori_loop(2, M, backward, 0)

    def weight(i, io):
        j = 2 * i + c
        for arr in (0, 1) if io == 0 else ():
            nh_send(i, arr).wait_recv()
            for m in range(M):
                e_send(i, arr, m).wait_recv()
        a, b = ((N.at[j], GP.at[j]), (H.at[j], GY.at[j + 1]))[io]
        g = dot_at(a[...].reshape(2 * OWN, C), b[...].reshape(2 * OWN, C))
        G[i, io] = g.astype(bf16).reshape(2, 8, 2, 16, C)

    xh_r, xh_l = ((x + 1) % 4) // 2, ((x + 3) % 4) // 2
    core = (c, 1 - c)

    def l1(io, e, side):
        return rc(
            G.at[xl, io, 1 - xh, pl.ds(side * 4, 4), core[e]], L1.at[io, e, side],
            p_s.at[io, e, side], p_r.at[io, e, side], (right, left)[side],
        )

    def l2(io, e, side, half):
        rows = pl.ds(half * 4, 4)
        return rc(
            G.at[1 - xl, io, (xh_r, xh_l)[side], rows, core[e]], L2.at[io, e, side, rows],
            q_s.at[io, e, side, half], q_r.at[io, e, side, half], (right, left)[side],
        )

    def first_sends(i, io):
        @pl.when(xl == i)
        def _():
            for e in range(2):
                l1(io, e, 0).start()
                l1(io, e, 1).start()

        @pl.when(xl != i)
        def _():
            for e in range(2):
                l2(io, e, 0, 1).start()
                l2(io, e, 1, 0).start()

    def relay(io, e):
        for side, xd in ((0, xh_r), (1, xh_l)):
            l1(io, e, side).wait_recv()
            rows = pl.ds(side * 4, 4)
            G[1 - xl, io, xd, rows, core[e]] = (
                G[1 - xl, io, xd, rows, core[e]].astype(f32) + L1[io, e, side].astype(f32)
            ).astype(bf16)
            l2(io, e, side, side).start()

    def z_send(io, e, off):
        return rc(
            T.at[io, e, (z + off) % 8], LZ.at[io, e, off],
            z_s.at[io, e, off], z_r.at[io, e, off], dev(x, y, (z + off) % 8, core[e]),
        )

    offs = ((4, 3, 5, 2, 6, 1, 7), (4, 3, 5, 2, 6, 1, 7, 0))

    def collect(io, e):
        for side in range(2):
            for half in range(2):
                l2(io, e, side, half).wait_recv()
        T[io, e] = (
            G[xl, io, xh, :, core[e]].astype(f32) + L2[io, e, 0].astype(f32) + L2[io, e, 1].astype(f32)
        ).astype(bf16)
        for off in offs[e]:
            z_send(io, e, off).start()

    weight(1, 0)
    first_sends(1, 0)
    weight(0, 0)
    first_sends(0, 0)
    weight(1, 1)
    weight(0, 1)
    relay(0, 0)
    relay(0, 1)
    first_sends(1, 1)
    first_sends(0, 1)
    pl.semaphore_wait(near_z.at[3], 2)
    collect(0, 0)
    collect(0, 1)
    relay(1, 0)
    relay(1, 1)
    collect(1, 0)
    collect(1, 1)

    for io in range(2):
        for e in range(2):
            total = T[io, 0, z].astype(f32) if e == 0 else 0.0
            for off in offs[e]:
                z_send(io, e, off).wait_recv()
                total = total + LZ[io, e, off].astype(f32)
            (gi_out, go_out)[io][core[e]] = total

    for t in range(4):
        for side in range(2):
            ag(t, side).wait_send()
        fw(t).wait_send()
    for t in SHARED:
        for side in range(2):
            zf(t, side).wait_send()

    @pl.when(y == 0)
    def _():
        for m in range(M):
            to_left(m).wait_send()
            to_right(m).wait_send()

    @pl.when((y > 0) & (y < 3))
    def _():
        for m in range(M):
            f_send(m).wait_send()

    @pl.when(y > 0)
    def _():
        for m in range(M):
            b_send(m).wait_send()

    for io in range(2):
        for i in range(2):
            nh_send(i, io).wait_send()
            for m in range(M):
                e_send(i, io, m).wait_send()
        for e in range(2):
            for side in range(2):
                l1(io, e, side).wait_send()
                for half in range(2):
                    l2(io, e, side, half).wait_send()
            for off in offs[e]:
                z_send(io, e, off).wait_send()


def local(images, out_grad, w_in, w_out):
    V = pltpu.VMEM
    REG = pltpu.SemaphoreType.REGULAR
    weights = V((4, C, C), bf16)
    acts = V((4, 2, M, R, C), bf16)
    wide = V((4, M, R, C), f32)
    scratch = [
        weights, weights, weights, weights,
        V((5, M, R, C), bf16), V((M, R, C), bf16), V((M, R, C), bf16),
        acts, acts, acts, V((5, 2, M, R, C), bf16), wide, wide, V((4, M, R, 128), f32),
        V((2, 2, 2, 8, 2, 16, C), bf16),
        V((2, 2, 2, 4, 16, C), bf16), V((2, 2, 2, 8, 16, C), bf16), V((2, 2, 8, 16, C), bf16),
        V((2, 2, 8, 16, C), bf16),
        DMA((2,)), DMA((UNITS,)), DMA((UNITS,)), DMA((4, 2)), DMA((4, 2)), DMA((4,)), DMA((4,)), DMA((4, 2)), DMA((4, 2)),
        DMA((M, 2)), DMA((M, 2)), DMA((M,)), DMA((M,)), DMA((M,)), DMA((M,)),
        DMA((2, 2)), DMA((2, 2)), DMA((2, 2, M)), DMA((2, 2, M)),
        DMA((2, 2, 2)), DMA((2, 2, 2)), DMA((2, 2, 2, 2)), DMA((2, 2, 2, 2)), DMA((2, 2, 8)), DMA((2, 2, 8)),
        REG((4,)), REG,
    ]
    out = jax.ShapeDtypeStruct((2, 16, C), f32)
    grad_in, grad_out = pl.pallas_call(
        kernel,
        out_shape=(out, out),
        in_specs=[pl.BlockSpec(memory_space=pltpu.HBM)] * 4,
        out_specs=(pl.BlockSpec(memory_space=pltpu.VMEM),) * 2,
        scratch_shapes=scratch,
        compiler_params=pltpu.CompilerParams(
            collective_id=0, has_side_effects=True, vmem_limit_bytes=60 * 2**20
        ),
        name="window",
    )(images, out_grad, w_in, w_out)
    return grad_in[None], grad_out[None]


def solution(mesh):
    return jax.shard_map(
        local,
        mesh=mesh,
        in_specs=(
            P(None, "dp", None),
            P(None, "dp", None),
            P("section", None, None, None),
            P("section", None, None, None),
        ),
        out_specs=(P("section", None, "dp", None), P("section", None, "dp", None)),
        check_vma=False,
    )
```

time: 100 us -> 94.6 us (0.946)
  Pallas kernels: 96.1 us -> 91.7 us
    pallas_call x1, Pallas kernels: 96.1 us -> 91.7 us  [local(): pl.pallas_call(kernel, out_shape=(out, out), in_specs=[pl.BlockSpec(memor...]
where the time goes in v3:
time: 94.6 us; the launch traced here: 94.4 us
  Pallas kernels  91.7 us (97%)
  local copies, waits for them, and re-layouts  2.14 us (2%)
    pallas_call x1, Pallas kernels, local(): pl.pallas_call(kernel, out_shape=(out, out), in_specs=[pl.BlockSpec(memor...  91.7 us
    unnamed x4, local copies, waits for them, and re-layouts  2.14 us

profile of v3, /device:TPU:1, one launch (start us, length us, event | category | flops | bytes accessed | tf_op | source)
XLA Modules:
  0.0 94.4 jit_solution(3925021937231811994)
XLA Ops:
  0.6 91.7 %window.1 = (f32[2,16,512]{2,1,0:T(8,128)}, f32[2,16,512]{2,1,0:T(8,128)}) custom-call(bf16[4,192,512]{2,1,0:T(8,128)(2,1)} %img.1, bf16[4,192,512]{2,1,0:T(8,128)(2,1)} %og.1, bf16[1,2,512,512]{3,2,1,0:T(8,128)(2,1)} %wi.1, bf16[1,2,512,512]{3,2,1,0:T(8,128)(2,1)} %wo.1), custom_call_target="tpu_custom_call" | custom-call | tf_op jit(solution)/shard_map/window/pallas_call | solution.py:543
  92.3 0.0 copy-start
  92.3 1.5 %copy.8 = f32[1,2,16,512]{3,2,1,0:T(8,128)} copy(f32[1,2,16,512]{3,2,1,0:T(8,128)} %bitcast.3) | data formatting | bytes 131072
  93.8 0.0 copy-done
  93.8 0.6 copy.9
Async XLA Ops:
  92.3 1.5 %copy-start = (f32[2,16,512]{2,1,0:T(8,128)S(1)}, f32[2,16,512]{2,1,0:T(8,128)}, u32[]{:S(2)}) copy-start(f32[2,16,512]{2,1,0:T(8,128)} %get-tuple-element.5) | copy-start | bytes 196612

commit v4 on v3

--- a/solution.py
+++ b/solution.py
@@ -29,9 +29,9 @@
 
 def kernel(
     img, og, wi, wo, gi_out, go_out,
-    WI, WO, WIT, WOT, X, XT, XO, N, H, GP, GY, D, PRE, RS, G, L1, L2, T, LZ,
+    WI, WO, WIT, WOT, X, XT, XO, N, H, GP, GY, D, PRE, RS, G, L1, L2, T, LZ, ZP, ZM, Q, LX,
     loc_w, loc_m, loc_x, ag_s, ag_r, fw_s, fw_r, zf_s, zf_r, g_s, g_r, f_s, f_r, b_s, b_r, n_s, n_r, e_s, e_r, p_s, p_r, q_s, q_r, z_s, z_r,
-    near_z, diag,
+    zp_s, zp_r, zm_s, zm_r, lx_s, lx_r, near_z, diag,
 ):
     sec = lax.axis_index("section")
     dp = lax.axis_index("dp")
@@ -178,7 +178,7 @@
         wide = xb.astype(f32)
         r = lax.rsqrt(jnp.mean(wide * wide, axis=-1, keepdims=True) + norm_epsilon)
         p = dot(xb, WI[j]) * r
-        s = 1.0 / (1.0 + jnp.exp(-p))
+        s = 0.5 * jnp.tanh(0.5 * p) + 0.5
         h = p * s
         hb = h.astype(bf16)
         if save:
@@ -392,7 +392,7 @@
 
     def weight(i, io):
         j = 2 * i + c
-        for arr in (0, 1) if io == 0 else ():
+        for arr in (0, 1) if io == 1 else ():
             nh_send(i, arr).wait_recv()
             for m in range(M):
                 e_send(i, arr, m).wait_recv()
@@ -416,18 +416,16 @@
             q_s.at[io, e, side, half], q_r.at[io, e, side, half], (right, left)[side],
         )
 
-    def first_sends(i, io):
+    def first_sends(i, io, e):
         @pl.when(xl == i)
         def _():
-            for e in range(2):
-                l1(io, e, 0).start()
-                l1(io, e, 1).start()
+            l1(io, e, 0).start()
+            l1(io, e, 1).start()
 
         @pl.when(xl != i)
         def _():
-            for e in range(2):
-                l2(io, e, 0, 1).start()
-                l2(io, e, 1, 0).start()
+            l2(io, e, 0, 1).start()
+            l2(io, e, 1, 0).start()
 
     def relay(io, e):
         for side, xd in ((0, xh_r), (1, xh_l)):
@@ -456,31 +454,69 @@
         for off in offs[e]:
             z_send(io, e, off).start()
 
+    def part(chunk):
+        return (slice(None), 1, slice(None), chunk, c)
+
+    def zp(n):
+        return rc(G.at[part((z + 4 - n) % 8)], ZP.at[n], zp_s.at[n], zp_r.at[n], ring_z(1))
+
+    def zm(n):
+        return rc(G.at[part((z + 5 + n) % 8)], ZM.at[n], zm_s.at[n], zm_r.at[n], ring_z(7))
+
+    def ring_step(n):
+        zp(n).wait_recv()
+        here = part((z + 3 - n) % 8)
+        G[here] = (G[here].astype(f32) + ZP[n].astype(f32)).astype(bf16)
+        zp(n + 1).start()
+        if n < 2:
+            zm(n).wait_recv()
+            here = part((z + 6 + n) % 8)
+            G[here] = (G[here].astype(f32) + ZM[n].astype(f32)).astype(bf16)
+            zm(n + 1).start()
+
+    def lx(off):
+        to = (x + off) % 4
+        return rc(Q.at[to % 2, to // 2], LX.at[off - 1], lx_s.at[off - 1], lx_r.at[off - 1], dev(to, y, z, c))
+
+    weight(1, 1)
+    first_sends(1, 1, 1)
+    weight(0, 1)
+    zp(0).start()
+    zm(0).start()
+    first_sends(0, 1, 1)
     weight(1, 0)
-    first_sends(1, 0)
+    first_sends(1, 0, 0)
     weight(0, 0)
-    first_sends(0, 0)
-    weight(1, 1)
-    weight(0, 1)
+    first_sends(0, 0, 0)
+    relay(1, 1)
+    first_sends(1, 0, 1)
+    first_sends(0, 0, 1)
+    ring_step(0)
+    pl.semaphore_wait(near_z.at[3], 2)
     relay(0, 0)
+    collect(1, 1)
+    ring_step(1)
     relay(0, 1)
-    first_sends(1, 1)
-    first_sends(0, 1)
-    pl.semaphore_wait(near_z.at[3], 2)
     collect(0, 0)
+    ring_step(2)
     collect(0, 1)
-    relay(1, 0)
-    relay(1, 1)
-    collect(1, 0)
-    collect(1, 1)
-
-    for io in range(2):
-        for e in range(2):
-            total = T[io, 0, z].astype(f32) if e == 0 else 0.0
-            for off in offs[e]:
-                z_send(io, e, off).wait_recv()
-                total = total + LZ[io, e, off].astype(f32)
-            (gi_out, go_out)[io][core[e]] = total
+    zp(3).wait_recv()
+    zm(2).wait_recv()
+    Q[...] = (G[part(z)].astype(f32) + ZP[3].astype(f32) + ZM[2].astype(f32)).astype(bf16)
+    for off in (2, 1, 3):
+        lx(off).start()
+
+    for io, e in ((1, 1), (0, 0), (0, 1)):
+        total = T[io, 0, z].astype(f32) if e == 0 else 0.0
+        for off in offs[e]:
+            z_send(io, e, off).wait_recv()
+            total = total + LZ[io, e, off].astype(f32)
+        (gi_out, go_out)[io][core[e]] = total
+    total = Q[xl, xh].astype(f32)
+    for off in range(1, 4):
+        lx(off).wait_recv()
+        total = total + LX[off - 1].astype(f32)
+    go_out[c] = total
 
     for t in range(4):
         for side in range(2):
@@ -511,13 +547,18 @@
             nh_send(i, io).wait_send()
             for m in range(M):
                 e_send(i, io, m).wait_send()
-        for e in range(2):
-            for side in range(2):
-                l1(io, e, side).wait_send()
-                for half in range(2):
-                    l2(io, e, side, half).wait_send()
-            for off in offs[e]:
-                z_send(io, e, off).wait_send()
+    for io, e in ((1, 1), (0, 0), (0, 1)):
+        for side in range(2):
+            l1(io, e, side).wait_send()
+            for half in range(2):
+                l2(io, e, side, half).wait_send()
+        for off in offs[e]:
+            z_send(io, e, off).wait_send()
+    for n in range(4):
+        zp(n).wait_send()
+    for n in range(3):
+        zm(n).wait_send()
+        lx(n + 1).wait_send()
 
 
 def local(images, out_grad, w_in, w_out):
@@ -533,10 +574,12 @@
         V((2, 2, 2, 8, 2, 16, C), bf16),
         V((2, 2, 2, 4, 16, C), bf16), V((2, 2, 2, 8, 16, C), bf16), V((2, 2, 8, 16, C), bf16),
         V((2, 2, 8, 16, C), bf16),
+        V((4, 2, 2, 16, C), bf16), V((3, 2, 2, 16, C), bf16), V((2, 2, 16, C), bf16), V((3, 16, C), bf16),
         DMA((2,)), DMA((UNITS,)), DMA((UNITS,)), DMA((4, 2)), DMA((4, 2)), DMA((4,)), DMA((4,)), DMA((4, 2)), DMA((4, 2)),
         DMA((M, 2)), DMA((M, 2)), DMA((M,)), DMA((M,)), DMA((M,)), DMA((M,)),
         DMA((2, 2)), DMA((2, 2)), DMA((2, 2, M)), DMA((2, 2, M)),
         DMA((2, 2, 2)), DMA((2, 2, 2)), DMA((2, 2, 2, 2)), DMA((2, 2, 2, 2)), DMA((2, 2, 8)), DMA((2, 2, 8)),
+        DMA((4,)), DMA((4,)), DMA((3,)), DMA((3,)), DMA((3,)), DMA((3,)),
         REG((4,)), REG,
     ]
     out = jax.ShapeDtypeStruct((2, 16, C), f32)

time: 94.6 us -> 91.8 us (0.970)
  Pallas kernels: 91.7 us -> 88 us
    pallas_call x1, Pallas kernels: 91.7 us -> 88 us  [local(): pl.pallas_call(kernel, out_shape=(out, out), in_specs=[pl.BlockSpec(memor...]
where the time goes in v4:
time: 91.8 us; the launch traced here: 90.8 us
  Pallas kernels  88 us (96%)
  local copies, waits for them, and re-layouts  2.14 us (2%)
    pallas_call x1, Pallas kernels, local(): pl.pallas_call(kernel, out_shape=(out, out), in_specs=[pl.BlockSpec(memor...  88 us
    unnamed x4, local copies, waits for them, and re-layouts  2.14 us

profile of v4, /device:TPU:1, one launch (start us, length us, event | category | flops | bytes accessed | tf_op | source)
XLA Modules:
  0.0 90.8 jit_solution(616939593923708021)
XLA Ops:
  0.6 88.0 %window.1 = (f32[2,16,512]{2,1,0:T(8,128)}, f32[2,16,512]{2,1,0:T(8,128)}) custom-call(bf16[4,192,512]{2,1,0:T(8,128)(2,1)} %img.1, bf16[4,192,512]{2,1,0:T(8,128)(2,1)} %og.1, bf16[1,2,512,512]{3,2,1,0:T(8,128)(2,1)} %wi.1, bf16[1,2,512,512]{3,2,1,0:T(8,128)(2,1)} %wo.1), custom_call_target="tpu_custom_call" | custom-call | tf_op jit(solution)/shard_map/window/pallas_call | solution.py:586
  88.7 0.0 copy-start
  88.7 1.5 %copy.8 = f32[1,2,16,512]{3,2,1,0:T(8,128)} copy(f32[1,2,16,512]{3,2,1,0:T(8,128)} %bitcast.3) | data formatting | bytes 131072
  90.2 0.0 copy-done
  90.2 0.6 copy.9
Async XLA Ops:
  88.7 1.5 %copy-start = (f32[2,16,512]{2,1,0:T(8,128)S(1)}, f32[2,16,512]{2,1,0:T(8,128)}, u32[]{:S(2)}) copy-start(f32[2,16,512]{2,1,0:T(8,128)} %get-tuple-element.5) | copy-start | bytes 196612

commit v5 on v4

--- a/solution.py
+++ b/solution.py
@@ -28,7 +28,7 @@
 
 
 def kernel(
-    img, og, wi, wo, gi_out, go_out,
+    img, og, wi, wo, out,
     WI, WO, WIT, WOT, X, XT, XO, N, H, GP, GY, D, PRE, RS, G, L1, L2, T, LZ, ZP, ZM, Q, LX,
     loc_w, loc_m, loc_x, ag_s, ag_r, fw_s, fw_r, zf_s, zf_r, g_s, g_r, f_s, f_r, b_s, b_r, n_s, n_r, e_s, e_r, p_s, p_r, q_s, q_r, z_s, z_r,
     zp_s, zp_r, zm_s, zm_r, lx_s, lx_r, near_z, diag,
@@ -205,37 +205,34 @@
     def to_up_right(m):
         return rc(XO.at[m], X.at[0, m], g_s.at[m, 1], f_r.at[m], up_right)
 
-    def first_row(m, carry):
-        @pl.when(xl == 1)
-        def _():
-            to_right(m).wait_recv()
-
+    def own_stream(m):
         xb = X[mine, m]
         for i in range(2):
             xb = cell(xb, mine + i, m)
             X[mine + i + 1, m] = xb
 
-        @pl.when(xl == 0)
-        def _():
-            to_left(m).start()
-
-        @pl.when(xl == 1)
-        def _():
-            to_up(m).start()
-            to_left(m).wait_recv()
-
+    def partner_stream(m):
         xb = XT[m]
         for i in range(2):
             xb = cell(xb, mine + i, m, save=False)
         XO[m] = xb
 
+    def first_row(m, carry):
         @pl.when(xl == 0)
         def _():
+            own_stream(m)
+            to_left(m).start()
+            partner_stream(m)
             to_right(m).start()
 
         @pl.when(xl == 1)
         def _():
+            to_left(m).wait_recv()
+            partner_stream(m)
             to_up_right(m).start()
+            to_right(m).wait_recv()
+            own_stream(m)
+            to_up(m).start()
 
         return carry
 
@@ -511,12 +508,12 @@
         for off in offs[e]:
             z_send(io, e, off).wait_recv()
             total = total + LZ[io, e, off].astype(f32)
-        (gi_out, go_out)[io][core[e]] = total
+        out[io, core[e]] = total
     total = Q[xl, xh].astype(f32)
     for off in range(1, 4):
         lx(off).wait_recv()
         total = total + LX[off - 1].astype(f32)
-    go_out[c] = total
+    out[1, c] = total
 
     for t in range(4):
         for side in range(2):
@@ -582,19 +579,18 @@
         DMA((4,)), DMA((4,)), DMA((3,)), DMA((3,)), DMA((3,)), DMA((3,)),
         REG((4,)), REG,
     ]
-    out = jax.ShapeDtypeStruct((2, 16, C), f32)
-    grad_in, grad_out = pl.pallas_call(
+    grads = pl.pallas_call(
         kernel,
-        out_shape=(out, out),
+        out_shape=jax.ShapeDtypeStruct((2, 2, 16, C), f32),
         in_specs=[pl.BlockSpec(memory_space=pltpu.HBM)] * 4,
-        out_specs=(pl.BlockSpec(memory_space=pltpu.VMEM),) * 2,
+        out_specs=pl.BlockSpec(memory_space=pltpu.VMEM),
         scratch_shapes=scratch,
         compiler_params=pltpu.CompilerParams(
             collective_id=0, has_side_effects=True, vmem_limit_bytes=60 * 2**20
         ),
         name="window",
     )(images, out_grad, w_in, w_out)
-    return grad_in[None], grad_out[None]
+    return grads[0][None], grads[1][None]
 
 
 def solution(mesh):

time: 91.8 us -> 91.1 us (level)
    unnamed x4 -> x0, local copies, waits for them, and re-layouts: 2.14 us -> none
    slice x0 -> x1, local copies, waits for them, and re-layouts: none -> 1.53 us  [local(): return (grads[0][None], grads[1][None])]
where the time goes in v5:
time: 91.1 us; the launch traced here: 90.4 us
  Pallas kernels  88.3 us (97%)
  local copies, waits for them, and re-layouts  1.53 us (2%)
    pallas_call x1, Pallas kernels, local(): pl.pallas_call(kernel, out_shape=jax.ShapeDtypeStruct((2, 2, 16, C), f32)...  88.3 us

profile of v5, /device:TPU:1, one launch (start us, length us, event | category | flops | bytes accessed | tf_op | source)
XLA Modules:
  0.0 90.4 jit_solution(4747733971243512056)
XLA Ops:
  0.6 88.3 %window.1 = f32[2,2,16,512]{3,2,1,0:T(8,128)} custom-call(bf16[4,192,512]{2,1,0:T(8,128)(2,1)} %img.1, bf16[4,192,512]{2,1,0:T(8,128)(2,1)} %og.1, bf16[1,2,512,512]{3,2,1,0:T(8,128)(2,1)} %wi.1, bf16[1,2,512,512]{3,2,1,0:T(8,128)(2,1)} %wo.1), custom_call_target="tpu_custom_call" | custom-call | tf_op jit(solution)/shard_map/window/pallas_call | solution.py:582
  88.9 1.5 %fusion = (f32[1,2,16,512]{3,2,1,0:T(8,128)}, f32[1,2,16,512]{3,2,1,0:T(8,128)}) fusion(f32[2,2,16,512]{3,2,1,0:T(8,128)} %window.1), kind=kLoop, calls=%fused_computation | loop fusion | bytes 262144 | tf_op jit(solution)/shard_map/slice | solution.py:593

commit v6 on v5

--- a/solution.py
+++ b/solution.py
@@ -9,8 +9,8 @@
 f32, bf16 = jnp.float32, jnp.bfloat16
 MESH = pl.DeviceIdType.MESH
 C = 512
-M = 4
-R = 96
+M = 6
+R = 64
 BATCH = 2
 OWN = M * R
 UNIT = 96 if R % 96 == 0 else (48 if R == 48 else 32)

time: 91.1 us -> 89.7 us (0.985)
  Pallas kernels: 88.3 us -> 86.3 us
    pallas_call x1, Pallas kernels: 88.3 us -> 86.3 us  [local(): pl.pallas_call(kernel, out_shape=jax.ShapeDtypeStruct((2, 2, 16, C), f32)...]
where the time goes in v6:
time: 89.7 us; the launch traced here: 88.5 us
  Pallas kernels  86.3 us (96%)
  local copies, waits for them, and re-layouts  1.53 us (2%)
    pallas_call x1, Pallas kernels, local(): pl.pallas_call(kernel, out_shape=jax.ShapeDtypeStruct((2, 2, 16, C), f32)...  86.3 us

profile of v6, /device:TPU:1, one launch (start us, length us, event | category | flops | bytes accessed | tf_op | source)
XLA Modules:
  0.0 88.5 jit_solution(1514825630892092187)
XLA Ops:
  0.6 86.3 %window.1 = f32[2,2,16,512]{3,2,1,0:T(8,128)} custom-call(bf16[4,192,512]{2,1,0:T(8,128)(2,1)} %img.1, bf16[4,192,512]{2,1,0:T(8,128)(2,1)} %og.1, bf16[1,2,512,512]{3,2,1,0:T(8,128)(2,1)} %wi.1, bf16[1,2,512,512]{3,2,1,0:T(8,128)(2,1)} %wo.1), custom_call_target="tpu_custom_call" | custom-call | tf_op jit(solution)/shard_map/window/pallas_call | solution.py:582
  86.9 1.5 %fusion = (f32[1,2,16,512]{3,2,1,0:T(8,128)}, f32[1,2,16,512]{3,2,1,0:T(8,128)}) fusion(f32[2,2,16,512]{3,2,1,0:T(8,128)} %window.1), kind=kLoop, calls=%fused_computation | loop fusion | bytes 262144 | tf_op jit(solution)/shard_map/slice | solution.py:593
